TPU v7x, 256 devices: a whole 4x4x8 slice. The times are simulated.
256 devices in a mesh: seq: 8 (over z), head: 4 (over y_hi, core), rep: 8 (over y_lo, x).
Axes of the slice: x: 4, y: 4 (y_hi: 2, y_lo: 2; y = y_hi * 2 + y_lo), z: 8, core: 2. Of those that a mesh axis runs over, the one named last changes fastest.
Arguments:
- queries: bfloat16 [8, 2048, 7168], P('rep', 'seq', 'head'), may hold values from -6 to 6
- new_keys: bfloat16 [8, 2048, 7168], P('rep', 'seq', 'head'), may hold values from -6 to 6
- new_values: bfloat16 [8, 2048, 7168], P('rep', 'seq', 'head'), may hold values from -4 to 4
- lengths: int32 [8, 4], P('rep'), may hold values from 1 to 1024, 2048 in all within a row
- offsets: int32 [8, 4], P('rep'), may hold values from 0 to 4095
- slot_map: int32 [8, 4], P('rep'), may hold values from 0 to 3, each once within a row
Outputs:
- attended: bfloat16 [8, 2048, 7168], P('rep', 'seq', 'head')
- key_cache: bfloat16 [8, 4, 1024, 7168], P('rep', 'head', None, 'seq')
- value_cache: bfloat16 [8, 4, 1024, 7168], P('rep', 'head', None, 'seq')
Inputs may be any that keep to these rules, and one draw needn't show every extreme that they name: `lengths`: each row sums to 2048; its first entry is the group's shared prompt; every row has one entry equal to 1024. `slot_map`: each row is a permutation of the group's requests.
All inputs are finite; a program needn't handle non-finite values.
Results may differ from a plain program's by a relative error of at most 0.011.
Values may be sent and summed in bfloat16 or wider, within the bound.
A program may use at most 128 MiB of HBM per device.

v0:
```python
import math

import jax
import jax.numpy as jnp
from jax import lax
from jax.sharding import PartitionSpec as P

HD = 224


NEG_FILL = -1e30
ROPE_BASE = 10000.0
KEY_BLOCK = 512


def rotate(source, places):
    full_width = source.shape[-1]
    half_width = full_width // 2
    inverse = jnp.power(
        jnp.float32(ROPE_BASE), -2.0 * jnp.arange(half_width, dtype=jnp.float32) / full_width
    )
    angles = places.astype(jnp.float32)[:, None] * inverse[None, :]
    cosine = jnp.cos(angles)[:, None, :]
    sine_terms = jnp.sin(angles)[:, None, :]
    first_part = source[..., :half_width].astype(jnp.float32)
    second_part = source[..., half_width:].astype(jnp.float32)
    rotated = jnp.concatenate(
        [
            first_part * cosine - second_part * sine_terms,
            second_part * cosine + first_part * sine_terms,
        ],
        axis=-1,
    )
    return rotated.astype(jnp.bfloat16)


def token_request(token_ids, ends_at):
    return jnp.sum((token_ids[:, None] >= ends_at[None, :]).astype(jnp.int32), axis=1)


def lookup_rows(request, lookup):
    matches = request[:, None] == jnp.arange(lookup.shape[0], dtype=jnp.int32)[None, :]
    return jnp.sum(jnp.where(matches, lookup[None, :], 0), axis=1)


def empty_state(head_count, row_count):
    return (
        jnp.full((head_count, row_count), NEG_FILL, jnp.float32),
        jnp.zeros((head_count, row_count), jnp.float32),
        jnp.zeros((head_count, row_count, HD), jnp.float32),
    )


def finish(running):
    row_best, row_total, summed = running
    head_count, row_count, _ = summed.shape
    return (
        (summed / row_total[:, :, None])
        .transpose(1, 0, 2)
        .reshape(row_count, head_count * HD)
        .astype(jnp.bfloat16)
    )


def update(
    running, query_token_rows, query_tok, query_req, key_rows, value_rows, key_start, ends_at
):
    row_count = key_rows.shape[0]
    head_count = query_token_rows.shape[1]
    key_token_index = key_start + jnp.arange(row_count, dtype=jnp.int32)
    key_req = token_request(key_token_index, ends_at)
    same_request = (key_req[None, :] == query_req[:, None]) & (
        key_token_index[None, :] <= query_tok[:, None]
    )
    prompt_keys = (key_req[None, :] == 0) & (query_req[:, None] != 0)
    allowed = same_request | prompt_keys
    row_best, row_total, summed = running
    key_head_stack = key_rows.reshape(row_count, head_count, HD)
    value_heads = value_rows.reshape(row_count, head_count, HD)
    scores = jnp.einsum(
        "ezq,izq->zei", query_token_rows, key_head_stack, preferred_element_type=jnp.float32
    ) * (1.0 / math.sqrt(HD))
    scores = jnp.where(allowed[None], scores, NEG_FILL)
    best_new = jnp.maximum(row_best, jnp.max(scores, axis=2))
    factor = jnp.exp(row_best - best_new)
    weights = jnp.where(allowed[None], jnp.exp(scores - best_new[:, :, None]), 0.0)
    total_new = row_total * factor + jnp.sum(weights, axis=2)
    mixed = jnp.einsum(
        "eva,ael->evl",
        weights.astype(jnp.bfloat16),
        value_heads,
        preferred_element_type=jnp.float32,
    )
    return (best_new, total_new, summed * factor[:, :, None] + mixed)


def per_device(queries, new_keys, new_values, lengths, offsets, slot_map):
    tok_dev = queries.shape[1]
    local_cols = queries.shape[2]
    head_count = local_cols // HD
    tokens_total = tok_dev * lax.axis_size("seq")
    cache_len = tokens_total // 2
    lengths_row = lengths[0]
    offsets_row = offsets[0]
    slots_row = slot_map[0]
    request_count = lengths_row.shape[0]
    ends_at = jnp.cumsum(lengths_row)
    begins = ends_at - lengths_row
    token_ids = lax.axis_index("seq") * tok_dev + jnp.arange(tok_dev, dtype=jnp.int32)
    request = token_request(token_ids, ends_at)
    places = lookup_rows(request, offsets_row) + token_ids - lookup_rows(request, begins)
    rot_queries = rotate(queries[0].reshape(tok_dev, head_count, HD), places)
    rot_keys = rotate(new_keys[0].reshape(tok_dev, head_count, HD), places).reshape(
        tok_dev, local_cols
    )
    value_rows = new_values[0]
    key_rows = lax.all_gather(rot_keys, "seq", axis=0, tiled=True)
    piece_values = lax.all_gather(value_rows, "seq", axis=0, tiled=True)
    row_count = key_rows.shape[0]

    def key_step(key_index, state_in):
        first_row = key_index * KEY_BLOCK
        return update(
            state_in,
            rot_queries,
            token_ids,
            request,
            lax.dynamic_slice_in_dim(key_rows, first_row, KEY_BLOCK, 0),
            lax.dynamic_slice_in_dim(piece_values, first_row, KEY_BLOCK, 0),
            first_row,
            ends_at,
        )

    finished = lax.fori_loop(0, row_count // KEY_BLOCK, key_step, empty_state(head_count, tok_dev))
    attended = finish(finished)
    stacked = jnp.stack([rot_keys, value_rows])
    my_slot = lax.axis_index("head")
    request_ids = jnp.arange(request_count, dtype=jnp.int32)
    owner = jnp.sum(jnp.where(slots_row == my_slot, request_ids, 0))
    owner_begin = jnp.sum(jnp.where(request_ids == owner, begins, 0))
    slot_of = lookup_rows(request, slots_row)
    member = slot_of[None, :] == request_ids[:, None]
    buckets = jnp.where(member[None, :, :, None], stacked[:, None], jnp.zeros((), jnp.bfloat16))
    moved = lax.all_to_all(
        lax.all_to_all(buckets, "head", split_axis=1, concat_axis=3, tiled=True),
        "seq",
        split_axis=3,
        concat_axis=2,
        tiled=True,
    )
    padded = jnp.concatenate(
        [moved, jnp.zeros((2, 1, cache_len, moved.shape[3]), jnp.bfloat16)], axis=2
    )
    window = lax.dynamic_slice_in_dim(padded, owner_begin, cache_len, 2)
    return (attended[None], window[0:1], window[1:2])


def solution(mesh):
    in_specs = (
        P("rep", "seq", "head"),
        P("rep", "seq", "head"),
        P("rep", "seq", "head"),
        P("rep", None),
        P("rep", None),
        P("rep", None),
    )
    out_specs = (
        P("rep", "seq", "head"),
        P("rep", "head", None, "seq"),
        P("rep", "head", None, "seq"),
    )
    return jax.shard_map(
        per_device, mesh=mesh, in_specs=in_specs, out_specs=out_specs, check_vma=False
    )
```

profile of v0, /device:TPU:96, one launch (start us, length us, event | category | flops | bytes accessed | tf_op | source)
XLA Modules:
  0.0 385.8 jit_solution(3452643616625133445)
XLA Ops:
  7.2 0.0 copy-start.2
  7.2 0.0 all-gather.4.cloned.1.call-start
  7.3 0.9 reduce-window.4
  8.1 0.7 fusion.29
  8.8 1.5 copy.46
  10.3 0.1 convert_reduce_fusion.1
  10.4 0.8 select_reduce_fusion
  11.1 0.5 multiply_cosine_fusion
  11.6 0.3 fusion.21
  11.9 1.0 maximum_convert_fusion
  12.9 0.0 all-gather.4.cloned.1.call-update
  12.9 0.0 all-gather.6.cloned.1.call-start
  13.0 1.3 copy.48
  14.3 0.0 all-gather.6.cloned.1.call-update
  14.3 0.6 copy.49
  14.9 1.4 pad_maximum_fusion
  16.3 2.8 copy.50
  19.1 3.4 broadcast_select_fusion
  22.6 5.6 %all-to-all-start = ((bf16[2,4,256,1792]{2,3,0,1:T(8,128)(2,1)}), bf16[2,4,256,1792]{2,3,0,1:T(8,128)(2,1)}, u32[]{:S(2)}, u32[]{:S(2)}) async-start(bf16[2,4,256,1792]{2,3,0,1:T(8,128)(2,1)} %broadcast_select_fusion), calls=%async_computation | async-start | bytes 14680064 | tf_op jit(solution)/shard_map/all_to_all | solution.py:145
  28.2 0.5 copy.47
  28.8 0.7 fusion.27
  29.5 1.3 fusion.28
  32.6 0.3 fusion.24
  32.9 0.1 pad_maximum_fusion.1
  33.0 78.6 %all-to-all-done = bf16[2,4,256,1792]{2,3,0,1:T(8,128)(2,1)} async-done(((bf16[2,4,256,1792]{2,3,0,1:T(8,128)(2,1)}), bf16[2,4,256,1792]{2,3,0,1:T(8,128)(2,1)}, u32[]{:S(2)}, u32[]{:S(2)}) %all-to-all-start) | async-done | bytes 7340064 | tf_op jit(solution)/shard_map/all_to_all | solution.py:145
  111.6 3.6 copy.51
  115.2 47.2 %copy.52 = bf16[2,1,256,7168]{2,0,1,3:T(2,128)(2,1)} copy(bf16[2,1,256,7168]{2,3,0,1:T(8,128)(2,1)S(1)} %bitcast.73) | data formatting | bytes 14680064 | tf_op jit(solution)/shard_map/all_to_all | solution.py:145
  162.3 7.7 %all-to-all-start.1 = ((bf16[2,1,256,7168]{2,0,1,3:T(2,128)(2,1)}), bf16[2,1,256,7168]{2,0,1,3:T(2,128)(2,1)}, u32[]{:S(2)}, u32[]{:S(2)}) async-start(bf16[2,1,256,7168]{2,0,1,3:T(2,128)(2,1)} %copy.52), calls=%async_computation.1 | async-start | bytes 14680064 | tf_op jit(solution)/shard_map/all_to_all | solution.py:144
  170.0 106.1 %all-gather.6.cloned.1.call-done = bf16[1,2048,1792]{1,2,0:T(8,128)(2,1)} async-done(((bf16[1,256,1792]{1,2,0:T(8,128)(2,1)}), bf16[1,2048,1792]{1,2,0:T(8,128)(2,1)}) %all-gather.6.cloned.1.call-update) | async-done | bytes 7340048 | tf_op jit(solution)/shard_map/all_gather | solution.py:118
  276.2 51.9 %while.18 = (s32[]{:T(128)}, f32[8,256]{1,0:T(8,128)S(1)}, f32[8,256]{1,0:T(8,128)S(1)}, f32[8,256,224]{1,2,0:T(8,128)}, s32[4]{0:T(128)S(1)}, /*index=5*/s32[25...) while((s32[]{:T(128)}, f32[8,256]{1,0:T(8,128)S(1)}, ...), condition=%wide.region_8.9_spmd.clone, body=%wide.region_4.8_spmd.clone.sunk | while | flops 955204608 | bytes 45631228 | solution.py:134
  276.2 0.1 convert_reduce_fusion.3
  276.3 0.3 and_or_fusion.2
  276.6 2.3 constant_dynamic-slice_fusion.3
  278.9 3.1 fusion.45
  281.9 3.3 fusion.46
  285.3 0.1 copy-done
  285.4 2.6 fusion.48
  288.0 0.1 convert_reduce_fusion.3
  288.1 0.3 and_or_fusion.2
  288.4 2.3 constant_dynamic-slice_fusion.3
  290.7 3.1 fusion.45
  293.8 3.3 fusion.46
  297.2 0.1 copy-done
  297.2 4.1 %fusion.48 = f32[8,256,224]{1,2,0:T(8,128)} fusion(f32[8,256,224]{1,2,0:T(8,128)} %get-tuple-element.350, bf16[512,8,224]{0,2,1:T(8,128)(2,1)S(1)} %bitcast.71, f32[8,512,256]{2,1,0:T(8,128)S(1)} %copy-done, f32[8,256]{1,0:T(8,128)S(1)} %select_maximum_fusion.2, pred[256,512]{0,1:T(8,128)(4,1)S(1)} %and_or_fusion.2, ...), kind=kOutput, calls=%fused_computation.13.clone.1 | convolution fusion | flops 476381184 | bytes 9846785 | tf_op jit(solution)/shard_map/while/body/eval_jaxpr/eva,ael->evl/dot_general | solution.py:88
  301.4 0.1 convert_reduce_fusion.3
  301.5 0.3 and_or_fusion.2
  301.8 2.3 constant_dynamic-slice_fusion.3
  304.1 3.1 fusion.45
  307.2 3.3 fusion.46
  310.5 0.1 copy-done
  310.6 4.1 %fusion.48 = f32[8,256,224]{1,2,0:T(8,128)} fusion(f32[8,256,224]{1,2,0:T(8,128)} %get-tuple-element.350, bf16[512,8,224]{0,2,1:T(8,128)(2,1)S(1)} %bitcast.71, f32[8,512,256]{2,1,0:T(8,128)S(1)} %copy-done, f32[8,256]{1,0:T(8,128)S(1)} %select_maximum_fusion.2, pred[256,512]{0,1:T(8,128)(4,1)S(1)} %and_or_fusion.2, ...), kind=kOutput, calls=%fused_computation.13.clone.1 | convolution fusion | flops 476381184 | bytes 9846785 | tf_op jit(solution)/shard_map/while/body/eval_jaxpr/eva,ael->evl/dot_general | solution.py:88
  314.7 0.1 convert_reduce_fusion.3
  314.8 0.3 and_or_fusion.2
  315.1 2.3 constant_dynamic-slice_fusion.3
  317.4 3.1 fusion.45
  320.5 3.3 fusion.46
  323.9 0.1 copy-done
  323.9 4.1 %fusion.48 = f32[8,256,224]{1,2,0:T(8,128)} fusion(f32[8,256,224]{1,2,0:T(8,128)} %get-tuple-element.350, bf16[512,8,224]{0,2,1:T(8,128)(2,1)S(1)} %bitcast.71, f32[8,512,256]{2,1,0:T(8,128)S(1)} %copy-done, f32[8,256]{1,0:T(8,128)S(1)} %select_maximum_fusion.2, pred[256,512]{0,1:T(8,128)(4,1)S(1)} %and_or_fusion.2, ...), kind=kOutput, calls=%fused_computation.13.clone.1 | convolution fusion | flops 476381184 | bytes 9846785 | tf_op jit(solution)/shard_map/while/body/eval_jaxpr/eva,ael->evl/dot_general | solution.py:88
  328.1 1.6 divide_convert_fusion
  329.7 1.4 copy.55
  331.1 24.2 %all-to-all-done.1 = bf16[2,1,256,7168]{2,0,1,3:T(2,128)(2,1)} async-done(((bf16[2,1,256,7168]{2,0,1,3:T(2,128)(2,1)}), bf16[2,1,256,7168]{2,0,1,3:T(2,128)(2,1)}, u32[]{:S(2)}, u32[]{:S(2)}) %all-to-all-start.1) | async-done | bytes 7340064 | tf_op jit(solution)/shard_map/all_to_all | solution.py:144
  355.3 7.0 %copy.53 = bf16[2,1,256,7168]{2,3,0,1:T(8,128)(2,1)} copy(bf16[2,1,256,7168]{2,0,1,3:T(2,128)(2,1)} %all-to-all-done.1) | data formatting | bytes 14680064 | tf_op jit(solution)/shard_map/all_to_all | solution.py:144
  362.3 11.1 %copy.54 = bf16[2,1,8,256,896]{4,3,2,0,1:T(8,128)(2,1)} copy(bf16[2,1,8,256,896]{3,4,2,0,1:T(8,128)(2,1)} %bitcast.74) | data formatting | bytes 14680064 | tf_op jit(solution)/shard_map/all_to_all | solution.py:144
  373.4 5.6 %fusion.19 = (bf16[1,1,1024,896]{3,2,1,0:T(8,128)(2,1)}, bf16[1,1,1024,896]{3,2,1,0:T(8,128)(2,1)}) fusion(s32[]{:T(128)S(6)} %add.111, s32[]{:T(128)S(6)} %select_n.53, bf16[2,1,2048,896]{3,2,0,1:T(8,128)(2,1)} %bitcast.75), kind=kLoop, calls=%fused_computation.32 | loop fusion | bytes 11010056
  (49 shorter events, 0.2 us)
Async XLA Ops:
  7.2 5.8 %copy-start.2 = (bf16[1,256,1792]{2,1,0:T(8,128)(2,1)S(1)}, bf16[1,256,1792]{2,1,0:T(8,128)(2,1)}, u32[]{:S(2)}) copy-start(bf16[1,256,1792]{2,1,0:T(8,128)(2,1)} %param.10) | copy-start | bytes 2752516
  7.2 162.8 %all-gather.4.cloned.1.call-start = ((), (), s32[]{:S(2)}) async-start(), calls=%async_computation.2 | async-start | bytes 8257536 | tf_op jit(solution)/shard_map/all_gather | solution.py:117
  12.9 1.4 copy-start.1
  12.9 263.2 %all-gather.6.cloned.1.call-start = ((), (), s32[]{:S(2)}) async-start(), calls=%async_computation.3 | async-start | bytes 8257536 | tf_op jit(solution)/shard_map/all_gather | solution.py:118
  22.6 5.6 %copy-start.3 = (bf16[1,256,1792]{2,1,0:T(8,128)(2,1)S(1)}, bf16[1,256,1792]{2,1,0:T(8,128)(2,1)}, u32[]{:S(2)}) copy-start(bf16[1,256,1792]{2,1,0:T(8,128)(2,1)} %param.8) | copy-start | bytes 2752516
  22.6 6.2 %copy-start.5 = (s32[1,4]{1,0:T(1,128)S(1)}, s32[1,4]{1,0:T(1,128)}, u32[]{:S(2)}) copy-start(s32[1,4]{1,0:T(1,128)} %param.13) | copy-start | bytes 52
  22.6 6.9 %copy-start.4 = (s32[1,4]{1,0:T(1,128)S(1)}, s32[1,4]{1,0:T(1,128)}, u32[]{:S(2)}) copy-start(s32[1,4]{1,0:T(1,128)} %param.11) | copy-start | bytes 52
  22.6 89.0 %all-to-all-start = ((bf16[2,4,256,1792]{2,3,0,1:T(8,128)(2,1)}), bf16[2,4,256,1792]{2,3,0,1:T(8,128)(2,1)}, u32[]{:S(2)}, u32[]{:S(2)}) async-start(bf16[2,4,256,1792]{2,3,0,1:T(8,128)(2,1)} %broadcast_select_fusion), calls=%async_computation | async-start | bytes 14680064 | tf_op jit(solution)/shard_map/all_to_all | solution.py:145
  162.3 192.9 %all-to-all-start.1 = ((bf16[2,1,256,7168]{2,0,1,3:T(2,128)(2,1)}), bf16[2,1,256,7168]{2,0,1,3:T(2,128)(2,1)}, u32[]{:S(2)}, u32[]{:S(2)}) async-start(bf16[2,1,256,7168]{2,0,1,3:T(2,128)(2,1)} %copy.52), calls=%async_computation.1 | async-start | bytes 14680064 | tf_op jit(solution)/shard_map/all_to_all | solution.py:144
  281.9 3.4 copy-start
  293.8 3.4 copy-start
  307.1 3.4 copy-start
  320.5 3.4 copy-start
Sparse Core Ops, SparseCore 0:
  13.1 91.4 all-gather.3
  106.8 169.2 all-gather.5
where the time goes:
time: 387 us; the launch traced here: 386 us
  waiting for transfers between devices  209 us (54%)
  local copies, waits for them, and re-layouts  92 us (24%)
  other arithmetic  28 us (7%)
  matrix products  27.3 us (7%)
  between operations  16.1 us (4%)
  starting transfers between devices  13.3 us (3%)
    all_gather x1, waiting for transfers between devices, per_device(): piece_values = lax.all_gather(value_rows, 'seq', axis=0, tiled=True)  106 us
    all_to_all x1, waiting for transfers between devices, per_device(): lax.all_to_all(buckets, 'head', split_axis=1, concat_axis=3, tiled=True)  78.6 us
    all_to_all x2, local copies, waits for them, and re-layouts, per_device(): lax.all_to_all(buckets, 'head', split_axis=1, concat_axis=3, tiled=True)  50.7 us
    all_to_all x1, waiting for transfers between devices, per_device(): lax.all_to_all(lax.all_to_all(buckets, 'head', split_axis=1, concat_axis=...  24.2 us
    all_to_all x2, local copies, waits for them, and re-layouts, per_device(): lax.all_to_all(lax.all_to_all(buckets, 'head', split_axis=1, concat_axis=...  18.1 us
    dot_general x4, matrix products, update(): jnp.einsum('eva,ael->evl', weights.astype(jnp.bfloat16), value_heads, pre...  15 us
    reduce_sum x4, other arithmetic, update(): total_new = row_total * factor + jnp.sum(weights, axis=2)  13.3 us
    dot_general x4, matrix products, update(): jnp.einsum('ezq,izq->zei', query_token_rows, key_head_stack, preferred_el...  12.3 us
  transfers between devices with their start and end apart: 4, of which 3 were waited for; matrix products, arithmetic and copies ran while one was open for 31% of the time, Pallas kernels for 0%

commit v1 on v0

v1 whole, which is shorter than its diff:
```python
import functools
import math

import jax
import jax.numpy as jnp
from jax import lax
from jax.experimental import pallas as pl
from jax.experimental.pallas import tpu as pltpu
from jax.sharding import PartitionSpec as P

HD = 224
HALF = HD // 2
ROPE_BASE = 10000.0
NEG_FILL = -1e30
MESH = pl.DeviceIdType.MESH
VMEM = pltpu.VMEM
STEPS = (4, 3, -3, 2, -2, 1, -1)
V, K, Q = 0, 1, 2


def rotate_kernel(v_ref, k_ref, q_ref, cos_ref, sin_ref, out_ref):
    cos, sin = cos_ref[...], sin_ref[...]
    for t, ref in ((V, v_ref), (K, k_ref), (Q, q_ref)):
        flipped = ref[...].T
        for i in range(4):
            if t == V:
                out_ref[t, i, 0] = flipped[i * HD : (i + 1) * HD]
            else:
                a = flipped[i * HD : i * HD + HALF].astype(jnp.float32)
                b = flipped[i * HD + HALF : (i + 1) * HD].astype(jnp.float32)
                out_ref[t, i, 0, :HALF] = (a * cos - b * sin).astype(jnp.bfloat16)
                out_ref[t, i, 0, HALF:] = (b * cos + a * sin).astype(jnp.bfloat16)


def rotated_blocks(queries, keys, values, cos, sin):
    tok = queries.shape[0]
    wide = pl.BlockSpec((tok, 4 * HD), lambda e: (0, e))
    table = pl.BlockSpec((HALF, tok), lambda e: (0, 0))
    return pl.pallas_call(
        rotate_kernel,
        grid=(2,),
        out_shape=jax.ShapeDtypeStruct((3, 4, 2, HD, tok), jnp.bfloat16),
        in_specs=[wide, wide, wide, table, table],
        out_specs=pl.BlockSpec((3, 4, 1, HD, tok), lambda e: (0, 0, e, 0, 0)),
        compiler_params=pltpu.CompilerParams(vmem_limit_bytes=48 << 20),
        name="rotate",
    )(values, keys, queries, cos, sin)


def exchange_kernel(
    x_ref, begin_ref, prompt_ref, kv_ref, out_ref,
    mid, rec, kn, osend,
    in_s, in_r, z_s, z_r, y_s, y_r, c_s, c_r, f_s, f_r, own_s, o_s, o_r,
):
    s, h, r = lax.axis_index("seq"), lax.axis_index("head"), lax.axis_index("rep")
    tok = rec.shape[-1]
    core, high = h % 2, h // 2
    c1 = high * 2 + (1 - core)
    y1 = (1 - high) * 2 + core
    y2 = (1 - high) * 2 + (1 - core)
    partners = (h, c1, y1, y2)
    o_self = s // 2 == h

    def remote(src, dst, send, recv, seq, head):
        return pltpu.make_async_remote_copy(
            src_ref=src, dst_ref=dst, send_sem=send, recv_sem=recv,
            device_id=(seq, head, r), device_id_type=MESH,
        )

    bar = pltpu.get_barrier_semaphore()
    for p in partners[1:]:
        pl.semaphore_signal(bar, inc=1, device_id=(s, p, r), device_id_type=MESH)
    for d in range(1, 8):
        pl.semaphore_signal(bar, inc=1, device_id=((s + d) % 8, h, r), device_id_type=MESH)
    for e in range(2):
        for p in range(4):
            here = (2 * h + e == s) & (p == h)

            @pl.when(jnp.logical_not(here))
            def _():
                pl.semaphore_signal(bar, inc=1, device_id=(2 * h + e, p, r), device_id_type=MESH)

    @pl.when(o_self)
    def _():
        pl.semaphore_wait(bar, 17)

    @pl.when(jnp.logical_not(o_self))
    def _():
        pl.semaphore_wait(bar, 18)

    def plane(t, rel, e):
        return remote(
            x_ref.at[t, partners[rel], e], mid.at[t, rel, e],
            in_s.at[t, rel, e], in_r.at[t, rel, e], s, partners[rel],
        )

    def plane_own(t, e):
        return pltpu.make_async_copy(x_ref.at[t, h, e], mid.at[t, 0, e], in_r.at[t, 0, e])

    for t in (V, K, Q):
        for e in range(2):
            plane(t, 2, e).start()
            plane(t, 3, e).start()
        for e in range(2):
            plane_own(t, e).start()
            plane(t, 1, e).start()

    def z_place(to):
        hs, e = to // 2, to % 2
        rel = (h % 2 + hs % 2) % 2 + 2 * ((h // 2 + hs // 2) % 2)
        return rel, e

    def z_issue(t):
        for n, d in enumerate(STEPS):
            to = (s + d + 8) % 8
            rel, e = z_place(to)
            pltpu.make_async_copy(mid.at[t, rel, e], mid.at[t, rel, e], in_r.at[t, rel, e]).wait()
            remote(mid.at[t, rel, e], rec.at[t, s], z_s.at[t, n], z_r.at[t, n], to, h).start()
        rel, e = z_place(s)
        pltpu.make_async_copy(mid.at[t, rel, e], mid.at[t, rel, e], in_r.at[t, rel, e]).wait()
        pltpu.make_async_copy(mid.at[t, rel, e], rec.at[t, s], z_r.at[t, 7]).start()

    def z_from(n):
        return s if n == 7 else (s - STEPS[n] + 8) % 8

    def z_wait(t, n):
        blk = z_from(n)
        pltpu.make_async_copy(rec.at[t, blk], rec.at[t, blk], z_r.at[t, n]).wait()
        return blk

    def share(t, n, blk):
        return (
            remote(rec.at[t, blk], kv_ref.at[t, blk, h], y_s.at[t, n], y_r.at[t, n], s, y1),
            remote(rec.at[t, blk], kv_ref.at[t, blk, h], c_s.at[t, n], c_r.at[t, n], s, c1),
            pltpu.make_async_copy(rec.at[t, blk], kv_ref.at[t, blk, h], own_s.at[t, n]),
        )

    def pass_on(t, n):
        blk = z_from(n)
        return remote(
            kv_ref.at[t, blk, y1], kv_ref.at[t, blk, y1], f_s.at[t, n], f_r.at[t, n], s, c1
        )

    def pass_wait(t, n):
        share(t, n, z_from(n))[0].wait_recv()
        pass_on(t, n).start()

    z_issue(V)
    z_issue(K)
    for n in (7, 0, 1, 2, 3, 4, 5, 6):
        blk = z_wait(V, n)
        for copy in share(V, n, blk):
            copy.start()
    z_issue(Q)
    for n in (7, 0, 1, 2, 3, 4, 5, 6):
        blk = z_wait(K, n)
        for copy in share(K, n, blk):
            copy.start()
        kn[blk] = rec[K, blk].T

    key_rel = lax.broadcasted_iota(jnp.int32, (tok, tok), 0)
    query_rel = lax.broadcasted_iota(jnp.int32, (tok, tok), 1)
    rate = math.log2(math.e) / math.sqrt(HD)
    prompt = prompt_ref[...]

    def attend(blk):
        q = rec[Q, blk]
        first = begin_ref[blk]

        def scores(j):
            raw = jnp.dot(kn[j], q, preferred_element_type=jnp.float32)
            place = key_rel + j * tok
            return raw, (place < prompt) | (place >= first)

        raw, seen = scores(blk)
        sc = jnp.where(seen & (key_rel <= query_rel), raw, NEG_FILL)
        best = jnp.max(sc, axis=0, keepdims=True)
        w = jnp.exp2((sc - best) * rate)
        total = jnp.sum(w, axis=0, keepdims=True)
        acc = jnp.dot(rec[V, blk], w.astype(jnp.bfloat16), preferred_element_type=jnp.float32)

        def step(j, state):
            best, total, acc = state
            raw, seen = scores(j)
            sc = jnp.where(seen, raw, NEG_FILL)
            new = jnp.maximum(best, jnp.max(sc, axis=0, keepdims=True))
            keep = jnp.exp2((best - new) * rate)
            w = jnp.exp2((sc - new) * rate)
            total = total * keep + jnp.sum(w, axis=0, keepdims=True)
            acc = acc * keep + jnp.dot(
                rec[V, j], w.astype(jnp.bfloat16), preferred_element_type=jnp.float32
            )
            return new, total, acc

        best, total, acc = lax.fori_loop(0, blk, step, (best, total, acc))
        osend[blk] = (acc / total).astype(jnp.bfloat16)

    mine = (s % 2) * 4 + h

    def give(blk, n):
        return remote(osend.at[blk], out_ref.at[mine], o_s.at[n], o_r.at[mine], blk, s // 2)

    def give_own():
        return pltpu.make_async_copy(osend.at[s], out_ref.at[mine], o_r.at[mine])

    for n in range(8):
        blk = z_wait(Q, n)
        attend(blk)
        if n < 7:
            give(blk, n).start()
        else:

            @pl.when(o_self)
            def _():
                give_own().start()

            @pl.when(jnp.logical_not(o_self))
            def _():
                give(blk, 7).start()

        pass_wait(V, (7, 0, 1, 2, 3, 4, 5, 6)[n])
    for n in (7, 0, 1, 2, 3, 4, 5, 6):
        pass_wait(K, n)

    for j in range(8):
        pltpu.make_async_copy(out_ref.at[j], out_ref.at[j], o_r.at[j]).wait()
    for t in (V, K):
        for n in range(8):
            yc, cc, oc = share(t, n, z_from(n))
            oc.wait()
            yc.wait_send()
            cc.wait()
            pass_on(t, n).wait()
    for t in (V, K, Q):
        for e in range(2):
            for rel in (1, 2, 3):
                plane(t, rel, e).wait_send()
        for n in range(7):
            remote(rec.at[t, s], rec.at[t, s], z_s.at[t, n], z_r.at[t, n], s, c1).wait_send()
    for n in range(7):
        give(z_from(n), n).wait_send()

    @pl.when(jnp.logical_not(o_self))
    def _():
        give(s, 7).wait_send()


def exchange(blocks, begin_rows, prompt_row):
    tok = blocks.shape[-1]
    seq = 2048 // tok
    dma = pltpu.SemaphoreType.DMA
    block = (HD, tok)
    return pl.pallas_call(
        exchange_kernel,
        out_shape=(
            jax.ShapeDtypeStruct((2, seq, 4) + block, jnp.bfloat16),
            jax.ShapeDtypeStruct((8,) + block, jnp.bfloat16),
        ),
        in_specs=[
            pl.BlockSpec(memory_space=pl.ANY),
            pl.BlockSpec(memory_space=VMEM),
            pl.BlockSpec(memory_space=VMEM),
        ],
        out_specs=(pl.BlockSpec(memory_space=pl.ANY), pl.BlockSpec(memory_space=pl.ANY)),
        scratch_shapes=[
            VMEM((3, 4, 2) + block, jnp.bfloat16),
            VMEM((3, seq) + block, jnp.bfloat16),
            VMEM((seq, tok, HD), jnp.bfloat16),
            VMEM((seq,) + block, jnp.bfloat16),
            dma((3, 4, 2)), dma((3, 4, 2)),
            dma((3, 8)), dma((3, 8)),
            dma((2, 8)), dma((2, 8)),
            dma((2, 8)), dma((2, 8)),
            dma((2, 8)), dma((2, 8)),
            dma((2, 8)),
            dma((8,)), dma((8,)),
        ],
        compiler_params=pltpu.CompilerParams(
            collective_id=0, has_side_effects=True, vmem_limit_bytes=56 << 20
        ),
        name="exchange",
    )(blocks, begin_rows, prompt_row)


def window_kernel(info_ref, lo_ref, hi_ref, cache_ref):
    p = pl.program_id(1)
    tok = lo_ref.shape[-1]
    shift, length = info_ref[1], info_ref[2]
    row = lax.broadcasted_iota(jnp.int32, (tok, tok), 0)
    col = lax.broadcasted_iota(jnp.int32, (tok, tok), 1)
    kept = row + p * tok < length
    low = jnp.where(kept & (col == row + shift), 1.0, 0.0).astype(jnp.bfloat16)
    high = jnp.where(kept & (col + tok == row + shift), 1.0, 0.0).astype(jnp.bfloat16)
    dims = (((1,), (1,)), ((), ()))
    cut = lax.dot_general(low, lo_ref[0, 0], dims, preferred_element_type=jnp.float32)
    cut += lax.dot_general(high, hi_ref[0, 0], dims, preferred_element_type=jnp.float32)
    cache_ref[0] = cut.astype(jnp.bfloat16)


def windows(info, kv):
    _, seq, rows, tok = kv.shape
    steps = seq // 2

    def low(t, p, info):
        return (t, jnp.minimum(info[0] + p, seq - 1), 0, 0)

    def high(t, p, info):
        return (t, jnp.minimum(info[0] + p + 1, seq - 1), 0, 0)

    return pl.pallas_call(
        window_kernel,
        grid_spec=pltpu.PrefetchScalarGridSpec(
            num_scalar_prefetch=1,
            grid=(2, steps),
            in_specs=[pl.BlockSpec((1, 1, rows, tok), low), pl.BlockSpec((1, 1, rows, tok), high)],
            out_specs=pl.BlockSpec((1, tok, rows), lambda t, p, info: (t, p, 0)),
        ),
        out_shape=jax.ShapeDtypeStruct((2, steps * tok, rows), jnp.bfloat16),
        name="windows",
    )(info, kv, kv)


def flip_kernel(x_ref, o_ref):
    o_ref[...] = x_ref[...].T


def flip(x):
    rows, tok = x.shape
    return pl.pallas_call(
        flip_kernel,
        grid=(2,),
        out_shape=jax.ShapeDtypeStruct((tok, rows), x.dtype),
        in_specs=[pl.BlockSpec((rows // 2, tok), lambda i: (i, 0))],
        out_specs=pl.BlockSpec((tok, rows // 2), lambda i: (0, i)),
        name="flip",
    )(x)


def per_device(queries, new_keys, new_values, lengths, offsets, slot_map):
    tok = queries.shape[1]
    seq = lax.axis_size("seq")
    lengths_row, offsets_row, slots_row = lengths[0], offsets[0], slot_map[0]
    ends = jnp.cumsum(lengths_row)
    begins = ends - lengths_row
    tokens = jnp.arange(tok * seq, dtype=jnp.int32)
    request = jnp.sum((tokens[:, None] >= ends[None, :]).astype(jnp.int32), axis=1)
    pick = request[:, None] == jnp.arange(4, dtype=jnp.int32)[None, :]
    begin_of = jnp.sum(jnp.where(pick, begins[None, :], 0), axis=1)
    place = jnp.sum(jnp.where(pick, (offsets_row - begins)[None, :], 0), axis=1) + tokens
    mine = lax.dynamic_slice_in_dim(place, lax.axis_index("seq") * tok, tok, 0)
    inverse = jnp.power(
        jnp.float32(ROPE_BASE), -2.0 * jnp.arange(HALF, dtype=jnp.float32) / HD
    )
    angles = inverse[:, None] * mine.astype(jnp.float32)[None, :]
    blocks = rotated_blocks(
        queries[0], new_keys[0], new_values[0], jnp.cos(angles), jnp.sin(angles)
    )
    begin_rows = begin_of.reshape(seq, 1, tok)
    prompt_row = jnp.broadcast_to(lengths_row[0], (1, tok))
    kv, attended = exchange(blocks, begin_rows, prompt_row)
    owner = slots_row == lax.axis_index("head")
    begin = jnp.sum(jnp.where(owner, begins, 0))
    length = jnp.sum(jnp.where(owner, lengths_row, 0))
    info = jnp.stack([begin // tok, begin % tok, length])
    caches = windows(info, kv.reshape(2, seq, 4 * HD, tok))
    return (flip(attended.reshape(8 * HD, tok))[None], caches[1][None, None], caches[0][None, None])


def solution(mesh):
    full = P("rep", "seq", "head")
    row = P("rep", None)
    cache = P("rep", "head", None, "seq")
    return jax.shard_map(
        per_device, mesh=mesh, in_specs=(full, full, full, row, row, row),
        out_specs=(full, cache, cache), check_vma=False,
    )
```

time: 387 us -> 136 us (0.35)
  the two profiles are of different devices: /device:TPU:96 before, /device:TPU:14 now
where the time goes in v1:
time: 136 us; the launch traced here: 135 us
  Pallas kernels  116 us (85%)
  local copies, waits for them, and re-layouts  10.5 us (8%)
  other arithmetic  5.37 us (4%)
  between operations  3.3 us (2%)
    pallas_call x1, Pallas kernels, exchange(): pl.pallas_call(exchange_kernel, out_shape=(jax.ShapeDtypeStruct((2, seq,...  103 us
    pallas_call x1, Pallas kernels, windows(): pl.pallas_call(window_kernel, grid_spec=pltpu.PrefetchScalarGridSpec(num_...  9.31 us
    unnamed x8, local copies, waits for them, and re-layouts  5.11 us
    another operation x1, local copies, waits for them, and re-layouts, per_device(): caches[0][None, None]  4.18 us

profile of v1, /device:TPU:14, one launch (start us, length us, event | category | flops | bytes accessed | tf_op | source)
XLA Modules:
  0.0 135.4 jit_solution(16135838399842695848)
XLA Ops:
  0.6 0.8 reduce-window.4
  1.5 1.3 fusion.1
  5.4 1.2 pad_add_fusion.info_ref
  6.6 1.2 broadcast_in_dim.46.prompt_ref
  7.8 0.7 subtract_bitcast_fusion
  8.5 0.1 convert_reduce_fusion
  8.6 0.7 select_reduce_fusion
  9.3 0.1 fusion
  9.4 0.5 multiply_sine_fusion
  9.8 0.0 copy-start.1
  9.8 1.2 copy-done.1
  11.0 0.0 copy-start.2
  11.0 1.2 copy-done.2
  12.2 0.0 copy-start.3
  12.2 1.2 copy-done.3
  13.4 1.4 %rotate.1.x_ref = bf16[3,4,2,224,256]{4,3,2,1,0:T(8,128)(2,1)S(1)} custom-call(bf16[256,1792]{1,0:T(8,128)(2,1)S(1)} %bitcast.41, bf16[256,1792]{1,0:T(8,128)(2,1)S(1)} %bitcast.42, bf16[256,1792]{1,0:T(8,128)(2,1)S(1)} %bitcast.43, f32[112,256]{1,0:T(8,128)S(1)} %get-tuple-element.14.cos_ref, f32[112,256]{1,0:T(8,128)S(1)} %get-tuple-element.13.sin_ref), custom_call_target="tpu_custom_call" | custom-call | tf_op jit(solution)/shard_map/rotate/pallas_call | solution.py:39
  14.8 0.0 copy-start
  14.8 1.6 %copy-done = bf16[3,4,2,224,256]{4,3,2,1,0:T(8,128)(2,1)} copy-done((bf16[3,4,2,224,256]{4,3,2,1,0:T(8,128)(2,1)}, bf16[3,4,2,224,256]{4,3,2,1,0:T(8,128)(2,1)S(1)}, u32[]{:S(2)}) %copy-start) | copy-done | bytes 2752536
  16.4 103.4 %exchange.1 = (bf16[2,8,4,224,256]{4,3,2,1,0:T(8,128)(2,1)}, bf16[8,224,256]{2,1,0:T(8,128)(2,1)}) custom-call(bf16[3,4,2,224,256]{4,3,2,1,0:T(8,128)(2,1)} %copy-done, s32[8,1,256]{2,1,0:T(1,128)} %bitcast.48, s32[1,256]{1,0:T(1,128)} %broadcast_in_dim.46.prompt_ref), custom_call_target="tpu_custom_call" | custom-call | tf_op jit(solution)/shard_map/exchange/pallas_call | solution.py:253
  119.8 2.2 %flip.1 = bf16[256,1792]{1,0:T(8,128)(2,1)} custom-call(bf16[1792,256]{1,0:T(8,128)(2,1)} %bitcast.47), custom_call_target="tpu_custom_call" | custom-call | tf_op jit(solution)/shard_map/flip/pallas_call | solution.py:329
  121.9 9.3 %windows.1 = bf16[2,1024,896]{2,1,0:T(8,128)(2,1)} custom-call(s32[3]{0:T(128)} %pad_add_fusion.info_ref, bf16[2,8,896,256]{3,2,1,0:T(8,128)(2,1)} %bitcast.44, bf16[2,8,896,256]{3,2,1,0:T(8,128)(2,1)} %bitcast.45), custom_call_target="tpu_custom_call" | custom-call | tf_op jit(solution)/shard_map/windows/pallas_call | solution.py:310
  131.3 4.2 %slice_bitcast_fusion = (bf16[1,1,1024,896]{3,2,1,0:T(8,128)(2,1)}, bf16[1,1,1024,896]{3,2,1,0:T(8,128)(2,1)}) fusion(bf16[2,1024,896]{2,1,0:T(8,128)(2,1)} %windows.1), kind=kLoop, calls=%fused_computation | loop fusion | bytes 7340032 | tf_op jit(solution)/shard_map/broadcast_in_dim;squeeze | solution.py:366
  (1 shorter events, 0.0 us)
Async XLA Ops:
  9.8 1.2 copy-start.1
  11.0 1.2 copy-start.2
  12.2 1.2 copy-start.3
  14.8 1.6 %copy-start = (bf16[3,4,2,224,256]{4,3,2,1,0:T(8,128)(2,1)}, bf16[3,4,2,224,256]{4,3,2,1,0:T(8,128)(2,1)S(1)}, u32[]{:S(2)}) copy-start(bf16[3,4,2,224,256]{4,3,2,1,0:T(8,128)(2,1)S(1)} %rotate.1.x_ref) | copy-start | bytes 8257540

commit v2 on v1

--- a/solution.py
+++ b/solution.py
@@ -16,9 +16,24 @@
 VMEM = pltpu.VMEM
 STEPS = (4, 3, -3, 2, -2, 1, -1)
 V, K, Q = 0, 1, 2
-
-
-def rotate_kernel(v_ref, k_ref, q_ref, cos_ref, sin_ref, out_ref):
+EXCHANGE_VMEM = 28 << 20
+FINISH_VMEM = 28 << 20
+
+
+def rotate_kernel(lens_ref, offs_ref, v_ref, k_ref, q_ref, rate_ref, out_ref, cos_ref, sin_ref):
+    @pl.when(pl.program_id(0) == 0)
+    def _():
+        tok = cos_ref.shape[-1]
+        token = lax.broadcasted_iota(jnp.int32, (1, tok), 1) + lax.axis_index("seq") * tok
+        ahead = jnp.full((1, tok), offs_ref[0, 0], jnp.int32)
+        end = lens_ref[0, 0]
+        for r in range(1, 4):
+            ahead = jnp.where(token >= end, offs_ref[0, r] - end, ahead)
+            end += lens_ref[0, r]
+        angles = rate_ref[...] * (token + ahead).astype(jnp.float32)
+        cos_ref[...] = jnp.cos(angles)
+        sin_ref[...] = jnp.sin(angles)
+
     cos, sin = cos_ref[...], sin_ref[...]
     for t, ref in ((V, v_ref), (K, k_ref), (Q, q_ref)):
         flipped = ref[...].T
@@ -32,23 +47,26 @@
                 out_ref[t, i, 0, HALF:] = (b * cos + a * sin).astype(jnp.bfloat16)
 
 
-def rotated_blocks(queries, keys, values, cos, sin):
+def rotated_blocks(lengths, offsets, queries, keys, values, rates):
     tok = queries.shape[0]
     wide = pl.BlockSpec((tok, 4 * HD), lambda e: (0, e))
-    table = pl.BlockSpec((HALF, tok), lambda e: (0, 0))
+    scalars = pl.BlockSpec(memory_space=pltpu.SMEM)
     return pl.pallas_call(
         rotate_kernel,
         grid=(2,),
         out_shape=jax.ShapeDtypeStruct((3, 4, 2, HD, tok), jnp.bfloat16),
-        in_specs=[wide, wide, wide, table, table],
+        in_specs=[
+            scalars, scalars, wide, wide, wide, pl.BlockSpec((HALF, 1), lambda e: (0, 0)),
+        ],
         out_specs=pl.BlockSpec((3, 4, 1, HD, tok), lambda e: (0, 0, e, 0, 0)),
+        scratch_shapes=[VMEM((HALF, tok), jnp.float32), VMEM((HALF, tok), jnp.float32)],
         compiler_params=pltpu.CompilerParams(vmem_limit_bytes=48 << 20),
         name="rotate",
-    )(values, keys, queries, cos, sin)
+    )(lengths, offsets, values, keys, queries, rates)
 
 
 def exchange_kernel(
-    x_ref, begin_ref, prompt_ref, kv_ref, out_ref,
+    x_ref, lens_ref, kv_ref, out_ref,
     mid, rec, kn, osend,
     in_s, in_r, z_s, z_r, y_s, y_r, c_s, c_r, f_s, f_r, own_s, o_s, o_r,
 ):
@@ -161,11 +179,17 @@
     key_rel = lax.broadcasted_iota(jnp.int32, (tok, tok), 0)
     query_rel = lax.broadcasted_iota(jnp.int32, (tok, tok), 1)
     rate = math.log2(math.e) / math.sqrt(HD)
-    prompt = prompt_ref[...]
+    prompt = lens_ref[0, 0]
+    token_rel = lax.broadcasted_iota(jnp.int32, (1, tok), 1)
 
     def attend(blk):
         q = rec[Q, blk]
-        first = begin_ref[blk]
+        token = token_rel + blk * tok
+        first = jnp.zeros_like(token)
+        end = 0
+        for r in range(3):
+            end += lens_ref[0, r]
+            first = jnp.where(token >= end, end, first)
 
         def scores(j):
             raw = jnp.dot(kn[j], q, preferred_element_type=jnp.float32)
@@ -245,7 +269,7 @@
         give(s, 7).wait_send()
 
 
-def exchange(blocks, begin_rows, prompt_row):
+def exchange(blocks, lengths):
     tok = blocks.shape[-1]
     seq = 2048 // tok
     dma = pltpu.SemaphoreType.DMA
@@ -258,8 +282,7 @@
         ),
         in_specs=[
             pl.BlockSpec(memory_space=pl.ANY),
-            pl.BlockSpec(memory_space=VMEM),
-            pl.BlockSpec(memory_space=VMEM),
+            pl.BlockSpec(memory_space=pltpu.SMEM),
         ],
         out_specs=(pl.BlockSpec(memory_space=pl.ANY), pl.BlockSpec(memory_space=pl.ANY)),
         scratch_shapes=[
@@ -276,94 +299,106 @@
             dma((8,)), dma((8,)),
         ],
         compiler_params=pltpu.CompilerParams(
-            collective_id=0, has_side_effects=True, vmem_limit_bytes=56 << 20
+            collective_id=0, has_side_effects=True, vmem_limit_bytes=EXCHANGE_VMEM
         ),
         name="exchange",
-    )(blocks, begin_rows, prompt_row)
-
-
-def window_kernel(info_ref, lo_ref, hi_ref, cache_ref):
-    p = pl.program_id(1)
-    tok = lo_ref.shape[-1]
-    shift, length = info_ref[1], info_ref[2]
+    )(blocks, lengths)
+
+
+def finish_kernel(
+    lens_ref, slots_ref, kv_ref, att_ref, out_ref, kc_ref, vc_ref,
+    att, flipped, kv, cut, att_s, in_s, cut_s,
+):
+    h = lax.axis_index("head")
+    seq, tok = kv_ref.shape[1], kv_ref.shape[3]
+    steps = seq // 2
+    begin, length, end = 0, 0, 0
+    for r in range(4):
+        mine = slots_ref[0, r] == h
+        begin = jnp.where(mine, end, begin)
+        length = jnp.where(mine, lens_ref[0, r], length)
+        end += lens_ref[0, r]
+    first, shift = begin // tok, begin % tok
+
+    def load(t, i):
+        blk = jnp.minimum(first + i, seq - 1)
+        return pltpu.make_async_copy(kv_ref.at[t, blk], kv.at[t, i], in_s.at[t, i])
+
+    def save(t, i):
+        to = (vc_ref, kc_ref)[t]
+        return pltpu.make_async_copy(cut.at[t, i], to.at[pl.ds(i * tok, tok)], cut_s.at[t, i])
+
+    take = pltpu.make_async_copy(att_ref, att, att_s.at[0])
+    give = pltpu.make_async_copy(flipped, out_ref, att_s.at[1])
+    take.start()
+    for i in range(steps + 1):
+        for t in (V, K):
+            load(t, i).start()
+    take.wait()
+    flipped[...] = att[...].T
     row = lax.broadcasted_iota(jnp.int32, (tok, tok), 0)
     col = lax.broadcasted_iota(jnp.int32, (tok, tok), 1)
-    kept = row + p * tok < length
-    low = jnp.where(kept & (col == row + shift), 1.0, 0.0).astype(jnp.bfloat16)
-    high = jnp.where(kept & (col + tok == row + shift), 1.0, 0.0).astype(jnp.bfloat16)
     dims = (((1,), (1,)), ((), ()))
-    cut = lax.dot_general(low, lo_ref[0, 0], dims, preferred_element_type=jnp.float32)
-    cut += lax.dot_general(high, hi_ref[0, 0], dims, preferred_element_type=jnp.float32)
-    cache_ref[0] = cut.astype(jnp.bfloat16)
-
-
-def windows(info, kv):
+    for t in (V, K):
+        load(t, 0).wait()
+    pending = give
+    for i in range(steps):
+        kept = row + i * tok < length
+        low = jnp.where(kept & (col == row + shift), 1.0, 0.0).astype(jnp.bfloat16)
+        high = jnp.where(kept & (col + tok == row + shift), 1.0, 0.0).astype(jnp.bfloat16)
+        for t in (V, K):
+            load(t, i + 1).wait()
+            part = lax.dot_general(low, kv[t, i], dims, preferred_element_type=jnp.float32)
+            part += lax.dot_general(high, kv[t, i + 1], dims, preferred_element_type=jnp.float32)
+            cut[t, i] = part.astype(jnp.bfloat16)
+            pending.start()
+            pending = save(t, i)
+    pending.start()
+    give.wait()
+    for i in range(steps):
+        for t in (V, K):
+            save(t, i).wait()
+
+
+def finish(lengths, slots, kv, attended):
     _, seq, rows, tok = kv.shape
+    wide = attended.shape[0]
     steps = seq // 2
-
-    def low(t, p, info):
-        return (t, jnp.minimum(info[0] + p, seq - 1), 0, 0)
-
-    def high(t, p, info):
-        return (t, jnp.minimum(info[0] + p + 1, seq - 1), 0, 0)
-
+    anywhere = pl.BlockSpec(memory_space=pl.ANY)
+    scalars = pl.BlockSpec(memory_space=pltpu.SMEM)
+    dma = pltpu.SemaphoreType.DMA
+    cache = jax.ShapeDtypeStruct((steps * tok, rows), jnp.bfloat16)
     return pl.pallas_call(
-        window_kernel,
-        grid_spec=pltpu.PrefetchScalarGridSpec(
-            num_scalar_prefetch=1,
-            grid=(2, steps),
-            in_specs=[pl.BlockSpec((1, 1, rows, tok), low), pl.BlockSpec((1, 1, rows, tok), high)],
-            out_specs=pl.BlockSpec((1, tok, rows), lambda t, p, info: (t, p, 0)),
-        ),
-        out_shape=jax.ShapeDtypeStruct((2, steps * tok, rows), jnp.bfloat16),
-        name="windows",
-    )(info, kv, kv)
-
-
-def flip_kernel(x_ref, o_ref):
-    o_ref[...] = x_ref[...].T
-
-
-def flip(x):
-    rows, tok = x.shape
-    return pl.pallas_call(
-        flip_kernel,
-        grid=(2,),
-        out_shape=jax.ShapeDtypeStruct((tok, rows), x.dtype),
-        in_specs=[pl.BlockSpec((rows // 2, tok), lambda i: (i, 0))],
-        out_specs=pl.BlockSpec((tok, rows // 2), lambda i: (0, i)),
-        name="flip",
-    )(x)
+        finish_kernel,
+        out_shape=(jax.ShapeDtypeStruct((tok, wide), jnp.bfloat16), cache, cache),
+        in_specs=[scalars, scalars, anywhere, anywhere],
+        out_specs=(anywhere, anywhere, anywhere),
+        scratch_shapes=[
+            VMEM((wide, tok), jnp.bfloat16),
+            VMEM((tok, wide), jnp.bfloat16),
+            VMEM((2, steps + 1, rows, tok), jnp.bfloat16),
+            VMEM((2, steps, tok, rows), jnp.bfloat16),
+            dma((2,)), dma((2, steps + 1)), dma((2, steps)),
+        ],
+        compiler_params=pltpu.CompilerParams(vmem_limit_bytes=FINISH_VMEM),
+        name="finish",
+    )(lengths, slots, kv, attended)
 
 
 def per_device(queries, new_keys, new_values, lengths, offsets, slot_map):
     tok = queries.shape[1]
     seq = lax.axis_size("seq")
-    lengths_row, offsets_row, slots_row = lengths[0], offsets[0], slot_map[0]
-    ends = jnp.cumsum(lengths_row)
-    begins = ends - lengths_row
-    tokens = jnp.arange(tok * seq, dtype=jnp.int32)
-    request = jnp.sum((tokens[:, None] >= ends[None, :]).astype(jnp.int32), axis=1)
-    pick = request[:, None] == jnp.arange(4, dtype=jnp.int32)[None, :]
-    begin_of = jnp.sum(jnp.where(pick, begins[None, :], 0), axis=1)
-    place = jnp.sum(jnp.where(pick, (offsets_row - begins)[None, :], 0), axis=1) + tokens
-    mine = lax.dynamic_slice_in_dim(place, lax.axis_index("seq") * tok, tok, 0)
-    inverse = jnp.power(
+    rates = jnp.power(
         jnp.float32(ROPE_BASE), -2.0 * jnp.arange(HALF, dtype=jnp.float32) / HD
     )
-    angles = inverse[:, None] * mine.astype(jnp.float32)[None, :]
     blocks = rotated_blocks(
-        queries[0], new_keys[0], new_values[0], jnp.cos(angles), jnp.sin(angles)
+        lengths, offsets, queries[0], new_keys[0], new_values[0], rates[:, None]
     )
-    begin_rows = begin_of.reshape(seq, 1, tok)
-    prompt_row = jnp.broadcast_to(lengths_row[0], (1, tok))
-    kv, attended = exchange(blocks, begin_rows, prompt_row)
-    owner = slots_row == lax.axis_index("head")
-    begin = jnp.sum(jnp.where(owner, begins, 0))
-    length = jnp.sum(jnp.where(owner, lengths_row, 0))
-    info = jnp.stack([begin // tok, begin % tok, length])
-    caches = windows(info, kv.reshape(2, seq, 4 * HD, tok))
-    return (flip(attended.reshape(8 * HD, tok))[None], caches[1][None, None], caches[0][None, None])
+    kv, attended = exchange(blocks, lengths)
+    out, keys, values = finish(
+        lengths, slot_map, kv.reshape(2, seq, 4 * HD, tok), attended.reshape(8 * HD, tok)
+    )
+    return out[None], keys[None, None], values[None, None]
 
 
 def solution(mesh):

time: 136 us -> 120 us (0.88)
  local copies, waits for them, and re-layouts: 10.5 us -> 4.85 us
  other arithmetic: 5.37 us -> 0.03 us
  between operations: 3.3 us -> 0.68 us
  Pallas kernels: 116 us -> 114 us
    another operation x1 -> x0, local copies, waits for them, and re-layouts: 4.18 us -> none  [per_device(): caches[0][None, None]]
    pallas_call x2 -> x1, Pallas kernels: 11.5 us -> 8.73 us  [finish(): pl.pallas_call(finish_kernel, out_shape=(jax.ShapeDtypeStruct((tok, wide)...]
    reduce_sum x3 -> x0, other arithmetic: 2.1 us -> none  [the longest x1 1.32 us: per_device(): begin = jnp.sum(jnp.where(owner, begins, 0))]
    another operation x2 -> x0, other arithmetic: 2.03 us -> none  [the longest x1 1.2 us: per_device(): info = jnp.stack([begin // tok, begin % tok, length])]
    unnamed x8 -> x12, local copies, waits for them, and re-layouts: 5.11 us -> 4.85 us
where the time goes in v2:
time: 120 us
  Pallas kernels  114 us (95%)
  local copies, waits for them, and re-layouts  4.85 us (4%)
    pallas_call x1, Pallas kernels, exchange(): pl.pallas_call(exchange_kernel, out_shape=(jax.ShapeDtypeStruct((2, seq,...  103 us
    pallas_call x1, Pallas kernels, finish(): pl.pallas_call(finish_kernel, out_shape=(jax.ShapeDtypeStruct((tok, wide)...  8.73 us
    unnamed x12, local copies, waits for them, and re-layouts  4.85 us

profile of v2, /device:TPU:14, one launch (start us, length us, event | category | flops | bytes accessed | tf_op | source)
XLA Modules:
  0.0 119.9 jit_solution(8900647975778340845)
XLA Ops:
  0.7 0.0 copy-start
  0.7 1.2 copy-done
  1.9 0.0 copy-start.1
  1.9 1.2 copy-done.1
  3.0 0.0 copy-start.2
  3.0 1.2 copy-done.2
  4.2 0.0 copy-start.3
  4.2 0.7 copy-done.3
  4.9 0.0 copy-start.4
  4.9 0.7 copy-done.4
  5.5 2.3 %rotate.1.x_ref = bf16[3,4,2,224,256]{4,3,2,1,0:T(8,128)(2,1)S(1)} custom-call(s32[1,4]{1,0:T(1,128)S(1)} %copy-done.3, s32[1,4]{1,0:T(1,128)S(1)} %copy-done.4, bf16[256,1792]{1,0:T(8,128)(2,1)S(1)} %bitcast.10, bf16[256,1792]{1,0:T(8,128)(2,1)S(1)} %bitcast.11, bf16[256,1792]{1,0:T(8,128)(2,1)S(1)} %bitcast.12, f32[112,1]{1,0:T(8,128)S(1)} %multiply_power_fusion.rate_ref), custom_call_target="tpu_custom_call" | custom-call | tf_op jit(solution)/shard_map/rotate/pallas_call | solution.py:54
  7.9 0.0 copy-start.5
  7.9 103.3 %exchange.1 = (bf16[2,8,4,224,256]{4,3,2,1,0:T(8,128)(2,1)S(1)}, bf16[8,224,256]{2,1,0:T(8,128)(2,1)S(1)}) custom-call(bf16[3,4,2,224,256]{4,3,2,1,0:T(8,128)(2,1)S(1)} %rotate.1.x_ref, s32[1,4]{1,0:T(1,128)S(1)} %copy-done.3), custom_call_target="tpu_custom_call" | custom-call | tf_op jit(solution)/shard_map/exchange/pallas_call | solution.py:277
  111.1 0.0 copy-done.5
  111.2 8.7 %finish.1 = (bf16[256,1792]{1,0:T(8,128)(2,1)}, bf16[1024,896]{1,0:T(8,128)(2,1)}, bf16[1024,896]{1,0:T(8,128)(2,1)}) custom-call(s32[1,4]{1,0:T(1,128)S(1)} %copy-done.3, s32[1,4]{1,0:T(1,128)S(1)} %copy-done.5, bf16[2,8,896,256]{3,2,1,0:T(8,128)(2,1)S(1)} %bitcast.8, bf16[1792,256]{1,0:T(8,128)(2,1)S(1)} %bitcast.9), custom_call_target="tpu_custom_call" | custom-call | tf_op jit(solution)/shard_map/finish/pallas_call | solution.py:371
  (1 shorter events, 0.0 us)
Async XLA Ops:
  0.7 1.2 copy-start
  1.9 1.2 copy-start.1
  3.0 1.2 copy-start.2
  4.2 0.7 copy-start.3
  4.9 0.7 copy-start.4
  7.9 103.3 %copy-start.5 = (s32[1,4]{1,0:T(1,128)S(1)}, s32[1,4]{1,0:T(1,128)}, u32[]{:S(2)}) copy-start(s32[1,4]{1,0:T(1,128)} %slots_ref.1) | copy-start | bytes 52

commit v3 on v2

--- a/solution.py
+++ b/solution.py
@@ -129,11 +129,18 @@
         return rel, e
 
     def z_issue(t):
-        for n, d in enumerate(STEPS):
-            to = (s + d + 8) % 8
-            rel, e = z_place(to)
+        def z_send(n, to, rel, e):
             pltpu.make_async_copy(mid.at[t, rel, e], mid.at[t, rel, e], in_r.at[t, rel, e]).wait()
             remote(mid.at[t, rel, e], rec.at[t, s], z_s.at[t, n], z_r.at[t, n], to, h).start()
+
+        for passes in ((0, 1) if t == V else (None,)):
+            for n, d in enumerate(STEPS):
+                to = (s + d + 8) % 8
+                rel, e = z_place(to)
+                if passes is None:
+                    z_send(n, to, rel, e)
+                else:
+                    pl.when(rel // 2 == passes)(functools.partial(z_send, n, to, rel, e))
         rel, e = z_place(s)
         pltpu.make_async_copy(mid.at[t, rel, e], mid.at[t, rel, e], in_r.at[t, rel, e]).wait()
         pltpu.make_async_copy(mid.at[t, rel, e], rec.at[t, s], z_r.at[t, 7]).start()
@@ -227,7 +234,7 @@
     def give_own():
         return pltpu.make_async_copy(osend.at[s], out_ref.at[mine], o_r.at[mine])
 
-    for n in range(8):
+    for n in (7, 0, 1, 2, 3, 4, 5, 6):
         blk = z_wait(Q, n)
         attend(blk)
         if n < 7:
@@ -242,7 +249,7 @@
             def _():
                 give(blk, 7).start()
 
-        pass_wait(V, (7, 0, 1, 2, 3, 4, 5, 6)[n])
+        pass_wait(V, n)
     for n in (7, 0, 1, 2, 3, 4, 5, 6):
         pass_wait(K, n)
 
@@ -306,8 +313,7 @@
 
 
 def finish_kernel(
-    lens_ref, slots_ref, kv_ref, att_ref, out_ref, kc_ref, vc_ref,
-    att, flipped, kv, cut, att_s, in_s, cut_s,
+    lens_ref, slots_ref, kv_ref, att_ref, out_ref, kc_ref, vc_ref, flipped, cut, out_s, cut_s,
 ):
     h = lax.axis_index("head")
     seq, tok = kv_ref.shape[1], kv_ref.shape[3]
@@ -320,36 +326,26 @@
         end += lens_ref[0, r]
     first, shift = begin // tok, begin % tok
 
-    def load(t, i):
-        blk = jnp.minimum(first + i, seq - 1)
-        return pltpu.make_async_copy(kv_ref.at[t, blk], kv.at[t, i], in_s.at[t, i])
+    def block(t, i):
+        return kv_ref[t, jnp.minimum(first + i, seq - 1)]
 
     def save(t, i):
         to = (vc_ref, kc_ref)[t]
         return pltpu.make_async_copy(cut.at[t, i], to.at[pl.ds(i * tok, tok)], cut_s.at[t, i])
 
-    take = pltpu.make_async_copy(att_ref, att, att_s.at[0])
-    give = pltpu.make_async_copy(flipped, out_ref, att_s.at[1])
-    take.start()
-    for i in range(steps + 1):
-        for t in (V, K):
-            load(t, i).start()
-    take.wait()
-    flipped[...] = att[...].T
+    give = pltpu.make_async_copy(flipped, out_ref, out_s)
+    flipped[...] = att_ref[...].T
     row = lax.broadcasted_iota(jnp.int32, (tok, tok), 0)
     col = lax.broadcasted_iota(jnp.int32, (tok, tok), 1)
     dims = (((1,), (1,)), ((), ()))
-    for t in (V, K):
-        load(t, 0).wait()
     pending = give
     for i in range(steps):
         kept = row + i * tok < length
         low = jnp.where(kept & (col == row + shift), 1.0, 0.0).astype(jnp.bfloat16)
         high = jnp.where(kept & (col + tok == row + shift), 1.0, 0.0).astype(jnp.bfloat16)
         for t in (V, K):
-            load(t, i + 1).wait()
-            part = lax.dot_general(low, kv[t, i], dims, preferred_element_type=jnp.float32)
-            part += lax.dot_general(high, kv[t, i + 1], dims, preferred_element_type=jnp.float32)
+            part = lax.dot_general(low, block(t, i), dims, preferred_element_type=jnp.float32)
+            part += lax.dot_general(high, block(t, i + 1), dims, preferred_element_type=jnp.float32)
             cut[t, i] = part.astype(jnp.bfloat16)
             pending.start()
             pending = save(t, i)
@@ -371,14 +367,14 @@
     return pl.pallas_call(
         finish_kernel,
         out_shape=(jax.ShapeDtypeStruct((tok, wide), jnp.bfloat16), cache, cache),
-        in_specs=[scalars, scalars, anywhere, anywhere],
+        in_specs=[
+            scalars, scalars, pl.BlockSpec(memory_space=VMEM), pl.BlockSpec(memory_space=VMEM),
+        ],
         out_specs=(anywhere, anywhere, anywhere),
         scratch_shapes=[
-            VMEM((wide, tok), jnp.bfloat16),
             VMEM((tok, wide), jnp.bfloat16),
-            VMEM((2, steps + 1, rows, tok), jnp.bfloat16),
             VMEM((2, steps, tok, rows), jnp.bfloat16),
-            dma((2,)), dma((2, steps + 1)), dma((2, steps)),
+            dma, dma((2, steps)),
         ],
         compiler_params=pltpu.CompilerParams(vmem_limit_bytes=FINISH_VMEM),
         name="finish",

time: 120 us -> 120 us (level)
  the two profiles are of different devices: /device:TPU:14 before, /device:TPU:69 now
where the time goes in v3:
time: 120 us
  Pallas kernels  114 us (95%)
  local copies, waits for them, and re-layouts  4.85 us (4%)
    pallas_call x1, Pallas kernels, exchange(): pl.pallas_call(exchange_kernel, out_shape=(jax.ShapeDtypeStruct((2, seq,...  107 us
    unnamed x12, local copies, waits for them, and re-layouts  4.85 us
    pallas_call x1, Pallas kernels, finish(): pl.pallas_call(finish_kernel, out_shape=(jax.ShapeDtypeStruct((tok, wide)...  4.24 us

profile of v3, /device:TPU:69, one launch (start us, length us, event | category | flops | bytes accessed | tf_op | source)
XLA Modules:
  0.0 119.6 jit_solution(2847661491872742419)
XLA Ops:
  0.7 0.0 copy-start
  0.7 1.2 copy-done
  1.9 0.0 copy-start.1
  1.9 1.2 copy-done.1
  3.0 0.0 copy-start.2
  3.0 1.2 copy-done.2
  4.2 0.0 copy-start.3
  4.2 0.7 copy-done.3
  4.9 0.0 copy-start.4
  4.9 0.7 copy-done.4
  5.5 2.3 %rotate.1.x_ref = bf16[3,4,2,224,256]{4,3,2,1,0:T(8,128)(2,1)S(1)} custom-call(s32[1,4]{1,0:T(1,128)S(1)} %copy-done.3, s32[1,4]{1,0:T(1,128)S(1)} %copy-done.4, bf16[256,1792]{1,0:T(8,128)(2,1)S(1)} %bitcast.10, bf16[256,1792]{1,0:T(8,128)(2,1)S(1)} %bitcast.11, bf16[256,1792]{1,0:T(8,128)(2,1)S(1)} %bitcast.12, f32[112,1]{1,0:T(8,128)S(1)} %multiply_power_fusion.rate_ref), custom_call_target="tpu_custom_call" | custom-call | tf_op jit(solution)/shard_map/rotate/pallas_call | solution.py:54
  7.9 0.0 copy-start.5
  7.9 107.5 %exchange.1 = (bf16[2,8,4,224,256]{4,3,2,1,0:T(8,128)(2,1)S(1)}, bf16[8,224,256]{2,1,0:T(8,128)(2,1)S(1)}) custom-call(bf16[3,4,2,224,256]{4,3,2,1,0:T(8,128)(2,1)S(1)} %rotate.1.x_ref, s32[1,4]{1,0:T(1,128)S(1)} %copy-done.3), custom_call_target="tpu_custom_call" | custom-call | tf_op jit(solution)/shard_map/exchange/pallas_call | solution.py:284
  115.3 0.0 copy-done.5
  115.4 4.2 %finish.1 = (bf16[256,1792]{1,0:T(8,128)(2,1)}, bf16[1024,896]{1,0:T(8,128)(2,1)}, bf16[1024,896]{1,0:T(8,128)(2,1)}) custom-call(s32[1,4]{1,0:T(1,128)S(1)} %copy-done.3, s32[1,4]{1,0:T(1,128)S(1)} %copy-done.5, bf16[2,8,896,256]{3,2,1,0:T(8,128)(2,1)S(1)} %bitcast.8, bf16[1792,256]{1,0:T(8,128)(2,1)S(1)} %bitcast.9), custom_call_target="tpu_custom_call" | custom-call | tf_op jit(solution)/shard_map/finish/pallas_call | solution.py:367
  (1 shorter events, 0.0 us)
Async XLA Ops:
  0.7 1.2 copy-start
  1.9 1.2 copy-start.1
  3.0 1.2 copy-start.2
  4.2 0.7 copy-start.3
  4.9 0.7 copy-start.4
  7.9 107.5 %copy-start.5 = (s32[1,4]{1,0:T(1,128)S(1)}, s32[1,4]{1,0:T(1,128)}, u32[]{:S(2)}) copy-start(s32[1,4]{1,0:T(1,128)} %slots_ref.1) | copy-start | bytes 52

commit v4 on v3

--- a/solution.py
+++ b/solution.py
@@ -129,18 +129,11 @@
         return rel, e
 
     def z_issue(t):
-        def z_send(n, to, rel, e):
+        for n, d in enumerate(STEPS):
+            to = (s + d + 8) % 8
+            rel, e = z_place(to)
             pltpu.make_async_copy(mid.at[t, rel, e], mid.at[t, rel, e], in_r.at[t, rel, e]).wait()
             remote(mid.at[t, rel, e], rec.at[t, s], z_s.at[t, n], z_r.at[t, n], to, h).start()
-
-        for passes in ((0, 1) if t == V else (None,)):
-            for n, d in enumerate(STEPS):
-                to = (s + d + 8) % 8
-                rel, e = z_place(to)
-                if passes is None:
-                    z_send(n, to, rel, e)
-                else:
-                    pl.when(rel // 2 == passes)(functools.partial(z_send, n, to, rel, e))
         rel, e = z_place(s)
         pltpu.make_async_copy(mid.at[t, rel, e], mid.at[t, rel, e], in_r.at[t, rel, e]).wait()
         pltpu.make_async_copy(mid.at[t, rel, e], rec.at[t, s], z_r.at[t, 7]).start()
@@ -234,7 +227,7 @@
     def give_own():
         return pltpu.make_async_copy(osend.at[s], out_ref.at[mine], o_r.at[mine])
 
-    for n in (7, 0, 1, 2, 3, 4, 5, 6):
+    for n in range(8):
         blk = z_wait(Q, n)
         attend(blk)
         if n < 7:
@@ -249,7 +242,7 @@
             def _():
                 give(blk, 7).start()
 
-        pass_wait(V, n)
+        pass_wait(V, (7, 0, 1, 2, 3, 4, 5, 6)[n])
     for n in (7, 0, 1, 2, 3, 4, 5, 6):
         pass_wait(K, n)
 

time: 120 us -> 116 us (0.967)
  the two profiles are of different devices: /device:TPU:69 before, /device:TPU:14 now
where the time goes in v4:
time: 116 us; the launch traced here: 115 us
  Pallas kernels  110 us (95%)
  local copies, waits for them, and re-layouts  4.85 us (4%)
    pallas_call x1, Pallas kernels, exchange(): pl.pallas_call(exchange_kernel, out_shape=(jax.ShapeDtypeStruct((2, seq,...  103 us
    unnamed x12, local copies, waits for them, and re-layouts  4.85 us
    pallas_call x1, Pallas kernels, finish(): pl.pallas_call(finish_kernel, out_shape=(jax.ShapeDtypeStruct((tok, wide)...  4.24 us
    pallas_call x1, Pallas kernels, rotated_blocks(): pl.pallas_call(rotate_kernel, grid=(2,), out_shape=jax.ShapeDtypeStruct((...  2.33 us

profile of v4, /device:TPU:14, one launch (start us, length us, event | category | flops | bytes accessed | tf_op | source)
XLA Modules:
  0.0 115.4 jit_solution(11121841383701618057)
XLA Ops:
  0.7 0.0 copy-start
  0.7 1.2 %copy-done = bf16[1,256,1792]{2,1,0:T(8,128)(2,1)S(1)} copy-done((bf16[1,256,1792]{2,1,0:T(8,128)(2,1)S(1)}, bf16[1,256,1792]{2,1,0:T(8,128)(2,1)}, u32[]{:S(2)}) %copy-start) | copy-done | bytes 917528
  1.9 0.0 copy-start.1
  1.9 1.2 %copy-done.1 = bf16[1,256,1792]{2,1,0:T(8,128)(2,1)S(1)} copy-done((bf16[1,256,1792]{2,1,0:T(8,128)(2,1)S(1)}, bf16[1,256,1792]{2,1,0:T(8,128)(2,1)}, u32[]{:S(2)}) %copy-start.1) | copy-done | bytes 917528
  3.0 0.0 copy-start.2
  3.0 1.2 %copy-done.2 = bf16[1,256,1792]{2,1,0:T(8,128)(2,1)S(1)} copy-done((bf16[1,256,1792]{2,1,0:T(8,128)(2,1)S(1)}, bf16[1,256,1792]{2,1,0:T(8,128)(2,1)}, u32[]{:S(2)}) %copy-start.2) | copy-done | bytes 917528
  4.2 0.0 copy-start.3
  4.2 0.7 copy-done.3
  4.9 0.0 copy-start.4
  4.9 0.7 copy-done.4
  5.5 2.3 %rotate.1.x_ref = bf16[3,4,2,224,256]{4,3,2,1,0:T(8,128)(2,1)S(1)} custom-call(s32[1,4]{1,0:T(1,128)S(1)} %copy-done.3, s32[1,4]{1,0:T(1,128)S(1)} %copy-done.4, bf16[256,1792]{1,0:T(8,128)(2,1)S(1)} %bitcast.10, bf16[256,1792]{1,0:T(8,128)(2,1)S(1)} %bitcast.11, bf16[256,1792]{1,0:T(8,128)(2,1)S(1)} %bitcast.12, f32[112,1]{1,0:T(8,128)S(1)} %multiply_power_fusion.rate_ref), custom_call_target="tpu_custom_call" | custom-call | tf_op jit(solution)/shard_map/rotate/pallas_call | solution.py:54
  7.9 0.0 copy-start.5
  7.9 103.3 %exchange.1 = (bf16[2,8,4,224,256]{4,3,2,1,0:T(8,128)(2,1)S(1)}, bf16[8,224,256]{2,1,0:T(8,128)(2,1)S(1)}) custom-call(bf16[3,4,2,224,256]{4,3,2,1,0:T(8,128)(2,1)S(1)} %rotate.1.x_ref, s32[1,4]{1,0:T(1,128)S(1)} %copy-done.3), custom_call_target="tpu_custom_call" | custom-call | tf_op jit(solution)/shard_map/exchange/pallas_call | solution.py:277
  111.1 0.0 copy-done.5
  111.2 4.2 %finish.1 = (bf16[256,1792]{1,0:T(8,128)(2,1)}, bf16[1024,896]{1,0:T(8,128)(2,1)}, bf16[1024,896]{1,0:T(8,128)(2,1)}) custom-call(s32[1,4]{1,0:T(1,128)S(1)} %copy-done.3, s32[1,4]{1,0:T(1,128)S(1)} %copy-done.5, bf16[2,8,896,256]{3,2,1,0:T(8,128)(2,1)S(1)} %bitcast.8, bf16[1792,256]{1,0:T(8,128)(2,1)S(1)} %bitcast.9), custom_call_target="tpu_custom_call" | custom-call | tf_op jit(solution)/shard_map/finish/pallas_call | solution.py:360
  (1 shorter events, 0.0 us)
Async XLA Ops:
  0.7 1.2 %copy-start = (bf16[1,256,1792]{2,1,0:T(8,128)(2,1)S(1)}, bf16[1,256,1792]{2,1,0:T(8,128)(2,1)}, u32[]{:S(2)}) copy-start(bf16[1,256,1792]{2,1,0:T(8,128)(2,1)} %param.8) | copy-start | bytes 2752516
  1.9 1.2 %copy-start.1 = (bf16[1,256,1792]{2,1,0:T(8,128)(2,1)S(1)}, bf16[1,256,1792]{2,1,0:T(8,128)(2,1)}, u32[]{:S(2)}) copy-start(bf16[1,256,1792]{2,1,0:T(8,128)(2,1)} %param.7) | copy-start | bytes 2752516
  3.0 1.2 %copy-start.2 = (bf16[1,256,1792]{2,1,0:T(8,128)(2,1)S(1)}, bf16[1,256,1792]{2,1,0:T(8,128)(2,1)}, u32[]{:S(2)}) copy-start(bf16[1,256,1792]{2,1,0:T(8,128)(2,1)} %param.6) | copy-start | bytes 2752516
  4.2 0.7 copy-start.3
  4.9 0.7 copy-start.4
  7.9 103.3 %copy-start.5 = (s32[1,4]{1,0:T(1,128)S(1)}, s32[1,4]{1,0:T(1,128)}, u32[]{:S(2)}) copy-start(s32[1,4]{1,0:T(1,128)} %slots_ref.1) | copy-start | bytes 52
